TPU v7x, 32 devices: a whole 2x2x4 slice. The times are simulated.
32 devices in a mesh: pool: 1, fsdp: 32 (over z, y, x, core).
Axes of the slice: x: 2, y: 2, z: 4, core: 2. Of those that a mesh axis runs over, the one named last changes fastest.
Arguments:
- noisy: bfloat16 [2048, 2560], P(('pool', 'fsdp')), may hold values from -6 to 6
- clean: bfloat16 [2048, 2560], P(('pool', 'fsdp')), may hold values from -6 to 6
- seg_ids: int32 [32], P('pool'), may hold values from 0 to 3, never falling along the last dimension, each value on 1 to 12 neighbouring positions
- lag_mask: int32 [32, 2], P(('pool', 'fsdp')), may hold values 0 or 1
- plan: int32 [32, 2], P(('pool', 'fsdp')), may hold values from 1 to 999, as said below
- w_query: bfloat16 [2560, 2560], P('fsdp'), may hold values from -0.125 to 0.125
- w_key: bfloat16 [2560, 2560], P('fsdp'), may hold values from -0.125 to 0.125
- time_proj: bfloat16 [128, 7680], replicated, may hold values from -0.5 to 0.5
- q_gain: float32 [2560], replicated, may hold values from 0.5 to 14
- k_gain: float32 [2560], replicated, may hold values from 0.5 to 14
Outputs:
- denoised: bfloat16 [2048, 2560], P(('pool', 'fsdp'))
Inputs may be any that keep to these rules, and one draw needn't show every extreme that they name: seg_ids never falls along the spans; each rollout is 1 to 12 consecutive spans. `plan`: entry j of a row lies from 1000 * (1 - j) // 2 + 1 to 1000 * (2 - j) // 2 - 1, so each row falls strictly.
All inputs are finite; a program needn't handle non-finite values. No bound on the sum of `lag_mask` on one device may be relied on, other than what follows from the above.
Results may differ from a plain program's by a relative error of at most 0.024.
Values may be sent and summed in bfloat16 or wider, within the bound.
No kernel may reach another device: no remote copies, remote signals or barrier semaphores. Data moves between devices by JAX's collectives and lax.ppermute only.
A program may use at most 128 MiB of HBM per device.

v0:
```python
import math
import jax
import jax.numpy as jnp
from jax import lax
from jax.sharding import PartitionSpec as P

HEADS = 20
HEAD_DIM = 128
STEPS = 2
LAGS = 2
LEVELS = 1000
SIGMA_SHIFT = 5.0
EPSILON = 1e-06
MASKED = -1e30


def passed_along(value, axis, steps):
    count = lax.axis_size(axis)
    leading, last = (max(0, -steps), min(count, count - steps))
    return lax.ppermute(value, axis, [(source, source + steps) for source in range(leading, last)])


def sigma_of(levels):
    fraction = levels.astype(jnp.float32) / LEVELS
    return SIGMA_SHIFT * fraction / (1.0 + (SIGMA_SHIFT - 1.0) * fraction)


def frequencies(half_count):
    return jnp.exp(-math.log(10000.0) * jnp.arange(half_count, dtype=jnp.float32) / half_count)


def modulation(sigmas, time_proj):
    half_count = time_proj.shape[0] // 2
    angles = 1000.0 * sigmas[:, None] * frequencies(half_count)[None, :]
    features = jnp.concatenate([jnp.cos(angles), jnp.sin(angles)], axis=1).astype(jnp.bfloat16)
    return jnp.dot(features, time_proj, preferred_element_type=jnp.float32)[0]


def modulate(latent, mod_row, model_width):
    values = latent.astype(jnp.float32)
    centred = values - jnp.mean(values, axis=-1, keepdims=True)
    variance = jnp.mean(centred * centred, axis=-1, keepdims=True)
    normed = centred * lax.rsqrt(variance + EPSILON)
    return (normed * (1.0 + mod_row[model_width : 2 * model_width]) + mod_row[:model_width]).astype(
        jnp.bfloat16
    )


def normalize(values, gain):
    mean_square = jnp.mean(values * values, axis=-1, keepdims=True)
    return values * lax.rsqrt(mean_square + EPSILON) * gain


def rotate(values, positions):
    half_count = HEAD_DIM // 2
    split_heads = values.reshape(values.shape[:-1] + (HEADS, HEAD_DIM))
    angles = positions[..., None] * frequencies(half_count)
    cosine = jnp.cos(angles)[..., None, :]
    sine = jnp.sin(angles)[..., None, :]
    front = split_heads[..., :half_count]
    back = split_heads[..., half_count:]
    turned = jnp.concatenate([front * cosine - back * sine, front * sine + back * cosine], axis=-1)
    return turned.reshape(values.shape)


def attend(query_rows, key_rows, value_rows, usable):
    row_count = query_rows.shape[0]
    query_heads = query_rows.reshape(row_count, HEADS, HEAD_DIM)
    key_heads = key_rows.reshape(-1, HEADS, HEAD_DIM)
    value_heads = value_rows.reshape(-1, HEADS, HEAD_DIM)
    scores = jnp.einsum(
        "qhd,khd->hqk", query_heads, key_heads, preferred_element_type=jnp.float32
    ) * HEAD_DIM ** (-0.5)
    scores = jnp.where(usable[None, None, :], scores, MASKED)
    highest = jnp.max(scores, axis=-1, keepdims=True)
    expanded = jnp.exp(scores - highest)
    weights = (expanded / jnp.sum(expanded, axis=-1, keepdims=True)).astype(jnp.bfloat16)
    mixed = jnp.einsum("hqk,khd->qhd", weights, value_heads, preferred_element_type=jnp.float32)
    return mixed.reshape(row_count, HEADS * HEAD_DIM).astype(jnp.bfloat16)


def make_absorbers(noisy_hidden, context_hidden):

    def absorb_both(carry, pieces, offset):
        stored = tuple((piece_rows for piece_rows in pieces))
        query_sum = jnp.dot(noisy_hidden, pieces[0], preferred_element_type=jnp.float32)
        key_sum = jnp.dot(noisy_hidden, pieces[1], preferred_element_type=jnp.float32)
        ctxkey_sum = jnp.dot(context_hidden, pieces[1], preferred_element_type=jnp.float32)
        return (stored, (query_sum, key_sum, ctxkey_sum))

    def absorb_key(carry, piece, offset):
        buffer_rows, partials = carry
        stored = lax.dynamic_update_slice_in_dim(buffer_rows, piece, offset, 0)
        key_sum, ctxkey_sum = partials
        key_sum = key_sum + jnp.dot(noisy_hidden, piece, preferred_element_type=jnp.float32)
        ctxkey_sum = ctxkey_sum + jnp.dot(context_hidden, piece, preferred_element_type=jnp.float32)
        return (stored, (key_sum, ctxkey_sum))

    def absorb_query(carry, piece, offset):
        buffer_rows, query_sum = carry
        stored = lax.dynamic_update_slice_in_dim(buffer_rows, piece, offset, 0)
        query_sum = query_sum + jnp.dot(noisy_hidden, piece, preferred_element_type=jnp.float32)
        return (stored, query_sum)

    return (absorb_both, absorb_key, absorb_query)


def local(noisy, clean, seg_ids, lag_mask, plan, w_query, w_key, time_proj, q_gain, k_gain):
    row_count, model_width = noisy.shape
    inner_width = w_query.shape[1]
    span_index = lax.axis_index("fsdp")
    segment_start = jnp.sum((seg_ids < seg_ids[span_index]).astype(jnp.int32))
    span_place = span_index - segment_start
    positions = (span_place * row_count + jnp.arange(row_count, dtype=jnp.int32)).astype(
        jnp.float32
    )
    sigmas = [sigma_of(plan[0, level_index : level_index + 1]) for level_index in range(STEPS)] + [
        jnp.zeros((1,), jnp.float32)
    ]
    rest_mod = modulation(jnp.zeros((1,), jnp.float32), time_proj)
    step_mods = [modulation(sigmas[level_index], time_proj) for level_index in range(STEPS)]
    context_hidden = modulate(clean, rest_mod, model_width)
    noisy_hidden = modulate(noisy, step_mods[0], model_width)
    absorb_both, absorb_key, absorb_query = make_absorbers(noisy_hidden, context_hidden)
    empty_buffer = jnp.zeros((model_width, inner_width), jnp.bfloat16)
    empty_sum = jnp.zeros((row_count, inner_width), jnp.float32)
    buffers, partials = absorb_both(
        ((empty_buffer, empty_buffer), (empty_sum, empty_sum, empty_sum)),
        (
            lax.all_gather(w_query, "fsdp", axis=0, tiled=True),
            lax.all_gather(w_key, "fsdp", axis=0, tiled=True),
        ),
        jnp.int32(0),
    )
    full_query, full_key = buffers
    query_sum, key_sum, ctxkey_sum = partials
    context_key = rotate(normalize(ctxkey_sum, k_gain), positions).astype(jnp.bfloat16)
    context_pair = jnp.stack([context_key, context_hidden])
    received = [passed_along(context_pair, "fsdp", 1)]
    distance = 2
    received.append(passed_along(context_pair, "fsdp", distance))
    usable_parts = [jnp.ones((row_count,), jnp.int32) > 0]
    for distance in range(1, LAGS + 1):
        source = jnp.maximum(span_index - distance, 0)
        allowed = (
            (span_index >= distance)
            & (seg_ids[source] == seg_ids[span_index])
            & (lag_mask[0, distance - 1] == 1)
        )
        usable_parts.append(jnp.broadcast_to(allowed, (row_count,)))
    usable = jnp.concatenate(usable_parts)
    keys_context = jnp.concatenate([pair_rows[0] for pair_rows in received], axis=0)
    values_context = jnp.concatenate([pair_rows[1] for pair_rows in received], axis=0)
    latent = noisy
    for step_index in range(STEPS):
        if step_index == 0:
            hidden = noisy_hidden
            query_raw, key_raw = (query_sum, key_sum)
        else:
            hidden = modulate(latent, step_mods[step_index], model_width)
            query_raw = jnp.dot(hidden, full_query, preferred_element_type=jnp.float32)
            key_raw = jnp.dot(hidden, full_key, preferred_element_type=jnp.float32)
        query_rows = rotate(normalize(query_raw, q_gain), positions).astype(jnp.bfloat16)
        key_rows = rotate(normalize(key_raw, k_gain), positions).astype(jnp.bfloat16)
        mixed = attend(
            query_rows,
            jnp.concatenate([key_rows, keys_context], axis=0),
            jnp.concatenate([hidden, values_context], axis=0),
            usable,
        )
        sigma_change = sigmas[step_index + 1] - sigmas[step_index]
        factor = sigma_change * step_mods[step_index][2 * model_width :]
        latent = (latent.astype(jnp.float32) + factor[None, :] * mixed.astype(jnp.float32)).astype(
            jnp.bfloat16
        )
    return latent


def solution(mesh):
    placed = (
        P(("pool", "fsdp"), None),
        P(("pool", "fsdp"), None),
        P("pool"),
        P(("pool", "fsdp"), None),
        P(("pool", "fsdp"), None),
        P("fsdp", None),
        P("fsdp", None),
        P(),
        P(),
        P(),
    )
    return jax.shard_map(
        local, mesh=mesh, in_specs=placed, out_specs=P(("pool", "fsdp"), None), check_vma=False
    )
```

profile of v0, /device:TPU:9, one launch (start us, length us, event | category | flops | bytes accessed | tf_op | source)
XLA Modules:
  0.0 298.8 jit_solution(1294598367972171601)
XLA Ops:
  8.0 1.3 fusion.99
  10.8 1.4 fusion.101
  12.2 2.0 fusion.50
  17.5 1.4 fusion.100
  21.0 1.1 convert_reduce_fusion.1
  22.2 1.1 convert_reduce_fusion.2
  23.3 1.2 fusion.30
  25.9 1.0 fusion.78
  26.9 82.3 %all-gather.3.cloned.1.call-done = bf16[2560,2560]{1,0:T(8,128)(2,1)} async-done(((bf16[80,2560]{1,0:T(8,128)(2,1)}), bf16[2560,2560]{1,0:T(8,128)(2,1)}) %all-gather.3.cloned.1.call-update) | async-done | bytes 13107216 | tf_op jit(solution)/shard_map/all_gather | solution.py:131
  109.2 7.4 %multiply_reduce_fusion.2 = (f32[64]{0:T(128)S(1)}, f32[64,2560]{1,0:T(8,128)S(1)}) fusion(bf16[2560,2560]{1,0:T(8,128)(2,1)} %all-gather.3.cloned.1.call-done, bf16[64,2560]{1,0:T(8,128)(2,1)S(1)} %copy-done.2, f32[2560]{0:T(1024)S(1)} %get-tuple-element.41, f32[2560]{0:T(1024)S(1)} %get-tuple-element.42, f32[64]{0:T(128)S(1)} %add_rsqrt_fusion.7, ...), kind=kOutput, calls=%fused_computation.79 | convolution fusion | flops 840171456 | bytes 14111488 | tf_op jit(solution)/shard_map/dot_general | solution.py:87
  116.6 1.0 copy-done.1
  117.6 2.5 multiply_reduce_fusion.4
  120.2 1.0 multiply_multiply_fusion.2
  121.2 1.0 reshape.305
  122.2 1.2 reshape.303
  123.3 2.8 fusion.95
  126.2 1.4 fusion.96
  127.5 80.8 %all-gather.5.cloned.1.call-done = bf16[2560,2560]{1,0:T(8,128)(2,1)} async-done(((bf16[80,2560]{1,0:T(8,128)(2,1)}), bf16[2560,2560]{1,0:T(8,128)(2,1)}) %all-gather.5.cloned.1.call-update) | async-done | bytes 13107216 | tf_op jit(solution)/shard_map/all_gather | solution.py:130
  208.3 7.3 %multiply_reduce_fusion.3 = (f32[64]{0:T(128)S(1)}, f32[64,2560]{1,0:T(8,128)S(1)}) fusion(bf16[2560,2560]{1,0:T(8,128)(2,1)} %all-gather.5.cloned.1.call-done, bf16[64,2560]{1,0:T(8,128)(2,1)S(1)} %copy-done.2, f32[2560]{0:T(1024)S(1)} %get-tuple-element.41, f32[2560]{0:T(1024)S(1)} %get-tuple-element.42, f32[64]{0:T(128)S(1)} %add_rsqrt_fusion.7, ...), kind=kOutput, calls=%fused_computation.83 | convolution fusion | flops 840171456 | bytes 14111488 | tf_op jit(solution)/shard_map/dot_general | solution.py:86
  215.6 1.0 multiply_multiply_fusion.3
  216.6 1.2 reshape.304
  218.1 0.8 copy-done.4
  219.6 1.8 subtract_convert_fusion.3
  222.4 0.9 pad_maximum_fusion.12
  223.3 3.2 %collective-permute-start = (bf16[2,64,2560]{2,1,0:T(8,128)(2,1)}, bf16[2,64,2560]{2,1,0:T(8,128)(2,1)S(1)}, u32[]{:S(2)}, u32[]{:S(2)}) collective-permute-start(bf16[2,64,2560]{2,1,0:T(8,128)(2,1)} %pad_maximum_fusion.12), channel_id=1, source_target_pairs={{0,1},{1,2},{2,3},{3,4},{4,5},{5,6},{6,7},{7,8},{8,9},{9,10},{10,1... | collective-permute-start | bytes 1966088 | tf_op jit(solution)/shard_map/ppermute | solution.py:20
  226.9 1.0 copy_bitcast_fusion.1
  228.0 3.3 %collective-permute-start.1 = (bf16[2,64,2560]{2,1,0:T(8,128)(2,1)}, bf16[2,64,2560]{2,1,0:T(8,128)(2,1)}, u32[]{:S(2)}, u32[]{:S(2)}) collective-permute-start(bf16[2,64,2560]{2,1,0:T(8,128)(2,1)} %pad_maximum_fusion.12), channel_id=1, source_target_pairs={{0,2},{1,3},{2,4},{3,5},{4,6},{5,7},{6,8},{7,9},{8,10},{9,11},{10,... | collective-permute-start | bytes 1966088 | tf_op jit(solution)/shard_map/ppermute | solution.py:20
  231.3 5.8 %collective-permute-done = bf16[2,64,2560]{2,1,0:T(8,128)(2,1)S(1)} collective-permute-done((bf16[2,64,2560]{2,1,0:T(8,128)(2,1)}, bf16[2,64,2560]{2,1,0:T(8,128)(2,1)S(1)}, u32[]{:S(2)}, u32[]{:S(2)}) %collective-permute-start) | collective-permute-done | bytes 655392 | tf_op jit(solution)/shard_map/ppermute | solution.py:20
  237.4 0.8 copy.31
  238.2 12.7 %collective-permute-done.1 = bf16[2,64,2560]{2,1,0:T(8,128)(2,1)} collective-permute-done((bf16[2,64,2560]{2,1,0:T(8,128)(2,1)}, bf16[2,64,2560]{2,1,0:T(8,128)(2,1)}, u32[]{:S(2)}, u32[]{:S(2)}) %collective-permute-start.1) | collective-permute-done | bytes 655392 | tf_op jit(solution)/shard_map/ppermute | solution.py:20
  250.9 1.8 fusion.98
  252.7 1.2 concatenate.89
  254.9 0.8 copy.25
  256.1 3.5 %fusion.102 = (f32[20,64]{1,0:T(8,128)S(1)}, f32[20,64,192]{2,1,0:T(8,128)}) fusion(bf16[64,20,128]{2,0,1:T(8,128)(2,1)} %copy.32, bf16[64,20,128]{2,0,1:T(8,128)(2,1)} %copy.31, bf16[64,20,64]{2,0,1:T(8,128)(2,1)} %get-tuple-element.33, bf16[64,20,64]{2,0,1:T(8,128)(2,1)} %get-tuple-element.34, pred[192]{0:T(512)(128)(4,1)S(1)} %copy-done.16, ...), kind=kOutput, calls=%fused_computation.168 | convolution fusion | flops 68485312 | bytes 2299072 | tf_op jit(solution)/shard_map/sub | solution.py:76
  259.5 1.9 fusion.11
  261.9 1.0 copy_bitcast_fusion
  262.9 7.3 %multiply_reduce_fusion = (f32[64]{0:T(128)S(1)}, f32[64,2560]{1,0:T(8,128)S(1)}) fusion(bf16[2560,2560]{1,0:T(8,128)(2,1)} %all-gather.3.cloned.1.call-done, bf16[64,2560]{1,0:T(8,128)(2,1)S(1)} %get-tuple-element.6, f32[2560]{0:T(1024)S(1)} %get-tuple-element.38, f32[2560]{0:T(1024)S(1)} %get-tuple-element.39, f32[64]{0:T(128)S(1)} %add_rsqrt_fusion.2, ...), kind=kOutput, calls=%fused_computation.71 | convolution fusion | flops 840171456 | bytes 14111488 | tf_op jit(solution)/shard_map/dot_general | solution.py:162
  270.2 1.0 multiply_multiply_fusion
  271.3 1.2 reshape.307
  272.4 1.4 fusion.93
  273.8 7.3 %multiply_reduce_fusion.1 = (f32[64]{0:T(128)S(1)}, f32[64,2560]{1,0:T(8,128)S(1)}) fusion(bf16[2560,2560]{1,0:T(8,128)(2,1)} %all-gather.5.cloned.1.call-done, bf16[64,2560]{1,0:T(8,128)(2,1)S(1)} %get-tuple-element.6, f32[2560]{0:T(1024)S(1)} %get-tuple-element.38, f32[2560]{0:T(1024)S(1)} %get-tuple-element.39, f32[64]{0:T(128)S(1)} %add_rsqrt_fusion.2, ...), kind=kOutput, calls=%fused_computation.75 | convolution fusion | flops 840171456 | bytes 14111488 | tf_op jit(solution)/shard_map/dot_general | solution.py:161
  281.1 1.0 multiply_multiply_fusion.1
  282.1 1.2 reshape.306
  283.6 0.8 copy-done.8
  284.7 1.2 subtract_convert_fusion.1
  285.9 3.2 %fusion.105 = (f32[20,64]{1,0:T(8,128)S(1)}, f32[20,64,192]{2,1,0:T(8,128)}) fusion(bf16[64,20,128]{2,0,1:T(8,128)(2,1)} %copy.32, bf16[64,20,128]{2,0,1:T(8,128)(2,1)} %copy.31, bf16[64,20,64]{2,0,1:T(8,128)(2,1)S(1)} %get-tuple-element.31, bf16[64,20,64]{2,0,1:T(8,128)(2,1)} %get-tuple-element.32, pred[192]{0:T(512)(128)(4,1)S(1)} %copy-done.16, ...), kind=kOutput, calls=%fused_computation.169 | convolution fusion | flops 68485312 | bytes 2299072 | tf_op jit(solution)/shard_map/sub | solution.py:76
  289.1 2.1 fusion.9
  291.2 0.8 fusion.39
  (76 shorter events, 8.5 us)
Async XLA Ops:
  6.5 18.3 %copy-start = (bf16[128,7680]{1,0:T(8,128)(2,1)S(1)}, bf16[128,7680]{1,0:T(8,128)(2,1)}, u32[]{:S(2)}) copy-start(bf16[128,7680]{1,0:T(8,128)(2,1)} %param.17) | copy-start | bytes 5898244
  6.5 18.0 %copy-start.3 = (bf16[64,2560]{1,0:T(8,128)(2,1)S(1)}, bf16[64,2560]{1,0:T(8,128)(2,1)}, u32[]{:S(2)}) copy-start(bf16[64,2560]{1,0:T(8,128)(2,1)} %param.11) | copy-start | bytes 983044
  6.5 102.6 %all-gather.3.cloned.1.call-start = ((), (), s32[]{:S(2)}) async-start(), calls=%async_computation | async-start | bytes 13516800 | tf_op jit(solution)/shard_map/all_gather | solution.py:131
  7.3 201.0 %all-gather.5.cloned.1.call-start = ((), (), s32[]{:S(2)}) async-start(), calls=%async_computation.1 | async-start | bytes 13516800 | tf_op jit(solution)/shard_map/all_gather | solution.py:130
  24.8 84.4 %copy-start.2 = (bf16[64,2560]{1,0:T(8,128)(2,1)S(1)}, bf16[64,2560]{1,0:T(8,128)(2,1)}, u32[]{:S(2)}) copy-start(bf16[64,2560]{1,0:T(8,128)(2,1)} %param.10) | copy-start | bytes 983044
  109.2 8.5 %copy-start.1 = (bf16[2560,2560]{1,0:T(8,128)(2,1)S(1)}, bf16[2560,2560]{1,0:T(8,128)(2,1)}, u32[]{:S(2)}) copy-start(bf16[2560,2560]{1,0:T(8,128)(2,1)} %all-gather.3.cloned.1.call-done) | copy-start | bytes 39321604
  117.6 2.6 copy-start.14
  127.5 88.1 %copy-start.15 = (f32[2560]{0:T(1024)S(1)}, f32[2560]{0:T(1024)}, u32[]{:S(2)}) copy-start(f32[2560]{0:T(1024)} %param.18) | copy-start | bytes 30724
  217.8 1.1 copy-start.4
  217.8 1.4 copy-start.5
  217.8 1.6 copy-start.6
  217.8 1.8 copy-start.7
  221.4 1.0 copy-start.10
  223.3 13.8 %collective-permute-start = (bf16[2,64,2560]{2,1,0:T(8,128)(2,1)}, bf16[2,64,2560]{2,1,0:T(8,128)(2,1)S(1)}, u32[]{:S(2)}, u32[]{:S(2)}) collective-permute-start(bf16[2,64,2560]{2,1,0:T(8,128)(2,1)} %pad_maximum_fusion.12), channel_id=1, source_target_pairs={{0,1},{1,2},{2,3},{3,4},{4,5},{5,6},{6,7},{7,8},{8,9},{9,10},{10,1... | collective-permute-start | bytes 1966088 | tf_op jit(solution)/shard_map/ppermute | solution.py:20
  228.0 22.9 %collective-permute-start.1 = (bf16[2,64,2560]{2,1,0:T(8,128)(2,1)}, bf16[2,64,2560]{2,1,0:T(8,128)(2,1)}, u32[]{:S(2)}, u32[]{:S(2)}) collective-permute-start(bf16[2,64,2560]{2,1,0:T(8,128)(2,1)} %pad_maximum_fusion.12), channel_id=1, source_target_pairs={{0,2},{1,3},{2,4},{3,5},{4,6},{5,7},{6,8},{7,9},{8,10},{9,11},{10,... | collective-permute-start | bytes 1966088 | tf_op jit(solution)/shard_map/ppermute | solution.py:20
  253.9 2.1 copy-start.16
  254.9 1.1 copy-start.11
  256.0 3.5 %copy-start.13 = (bf16[64,20,128]{2,0,1:T(8,128)(2,1)}, bf16[64,20,128]{2,0,1:T(8,128)(2,1)S(1)}, u32[]{:S(2)}) copy-start(bf16[64,20,128]{2,0,1:T(8,128)(2,1)S(1)} %copy.26) | copy-start | bytes 983044
  256.0 3.5 %copy-start.12 = (bf16[64,20,128]{2,0,1:T(8,128)(2,1)S(1)}, bf16[64,20,128]{2,0,1:T(8,128)(2,1)}, u32[]{:S(2)}) copy-start(bf16[64,20,128]{2,0,1:T(8,128)(2,1)} %copy.25) | copy-start | bytes 983044
  283.3 1.1 copy-start.8
  283.3 1.4 copy-start.9
Sparse Core Ops, SparseCore 0:
  10.2 98.9 all-gather.2
  112.0 96.2 all-gather.4
where the time goes:
time: 300 us; the launch traced here: 299 us
  waiting for transfers between devices  183 us (61%)
  matrix products  43.8 us (15%)
  local copies, waits for them, and re-layouts  26.6 us (9%)
  between operations  19.9 us (7%)
  other arithmetic  19.1 us (6%)
  starting transfers between devices  6.54 us (2%)
    all_gather x1, waiting for transfers between devices, local(): lax.all_gather(w_key, 'fsdp', axis=0, tiled=True)  82.3 us
    all_gather x1, waiting for transfers between devices, local(): lax.all_gather(w_query, 'fsdp', axis=0, tiled=True)  80.8 us
    ppermute x2, waiting for transfers between devices, passed_along(): lax.ppermute(value, axis, [(source, source + steps) for source in range(l...  18.6 us
    dot_general x1, matrix products, absorb_both(): jnp.dot(noisy_hidden, pieces[1], preferred_element_type=jnp.float32)  7.43 us
    dot_general x1, matrix products, local(): query_raw = jnp.dot(hidden, full_query, preferred_element_type=jnp.float32)  7.28 us
    dot_general x1, matrix products, absorb_both(): jnp.dot(noisy_hidden, pieces[0], preferred_element_type=jnp.float32)  7.28 us
    dot_general x1, matrix products, local(): key_raw = jnp.dot(hidden, full_key, preferred_element_type=jnp.float32)  7.28 us
    sub x2, matrix products, attend(): expanded = jnp.exp(scores - highest)  6.65 us
  transfers between devices with their start and end apart: 4, of which 4 were waited for; matrix products, arithmetic and copies ran while one was open for 11% of the time, Pallas kernels for 0%

commit v1 on v0

--- a/solution.py
+++ b/solution.py
@@ -127,7 +127,9 @@
     buffers, partials = absorb_both(
         ((empty_buffer, empty_buffer), (empty_sum, empty_sum, empty_sum)),
         (
-            lax.all_gather(w_query, "fsdp", axis=0, tiled=True),
+            jnp.concatenate(
+                lax.all_to_all(jnp.stack([w_query] * lax.axis_size("fsdp")), "fsdp", 0, 0), axis=0
+            ),
             lax.all_gather(w_key, "fsdp", axis=0, tiled=True),
         ),
         jnp.int32(0),

time: 300 us -> 449 us (1.50)
  waiting for transfers between devices: 183 us -> 328 us
  starting transfers between devices: 6.54 us -> 13.7 us
    all_gather x1, waiting for transfers between devices: 82.3 us -> 199 us  [local(): lax.all_gather(w_key, 'fsdp', axis=0, tiled=True)]
    all_to_all x0 -> x1, waiting for transfers between devices: none -> 112 us  [local(): lax.all_to_all(jnp.stack([w_query] * lax.axis_size('fsdp')), 'fsdp', 0, 0)]
    all_gather x1 -> x0, waiting for transfers between devices: 80.8 us -> none  [local(): lax.all_gather(w_query, 'fsdp', axis=0, tiled=True)]
    another operation x0 -> x1, local copies, waits for them, and re-layouts: none -> 7.2 us  [local(): jnp.stack([w_query] * lax.axis_size('fsdp'))]
    all_to_all x0 -> x1, starting transfers between devices: none -> 6.38 us  [local(): lax.all_to_all(jnp.stack([w_query] * lax.axis_size('fsdp')), 'fsdp', 0, 0)]
  transfers between devices with their start and end apart: 4 -> 4, of which waited for: 4 -> 4; matrix products, arithmetic and copies ran while one was open for 11% -> 8% of each run, Pallas kernels for 0% -> 0%
where the time goes in v1:
time: 449 us; the launch traced here: 444 us
  waiting for transfers between devices  328 us (73%)
  matrix products  43.5 us (10%)
  local copies, waits for them, and re-layouts  25.1 us (6%)
  between operations  19.4 us (4%)
  other arithmetic  14.7 us (3%)
  starting transfers between devices  13.7 us (3%)
    all_gather x1, waiting for transfers between devices, local(): lax.all_gather(w_key, 'fsdp', axis=0, tiled=True)  199 us
    all_to_all x1, waiting for transfers between devices, local(): lax.all_to_all(jnp.stack([w_query] * lax.axis_size('fsdp')), 'fsdp', 0, 0)  112 us
    ppermute x2, waiting for transfers between devices, passed_along(): lax.ppermute(value, axis, [(source, source + steps) for source in range(l...  15.2 us
  transfers between devices with their start and end apart: 4, of which 4 were waited for; matrix products, arithmetic and copies ran while one was open for 8% of the time, Pallas kernels for 0%

profile of v1, /device:TPU:9, one launch (start us, length us, event | category | flops | bytes accessed | tf_op | source)
XLA Modules:
  0.0 444.1 jit_solution(16683767625793898510)
XLA Ops:
  6.5 0.7 all-gather.2.cloned.1.call-update
  7.3 7.2 %stack.8 = bf16[32,80,2560]{2,1,0:T(8,128)(2,1)} broadcast(bf16[80,2560]{1,0:T(8,128)(2,1)} %param.15), dimensions={1,2} | broadcast | bytes 13516800 | tf_op jit(solution)/shard_map/stack | solution.py:131
  14.5 6.4 %all-to-all-start = ((bf16[32,80,2560]{2,1,0:T(8,128)(2,1)}), bf16[32,80,2560]{2,1,0:T(8,128)(2,1)}, u32[]{:S(2)}, u32[]{:S(2)}) async-start(bf16[32,80,2560]{2,1,0:T(8,128)(2,1)} %stack.8), calls=%async_computation | async-start | bytes 26214400 | tf_op jit(solution)/shard_map/all_to_all | solution.py:131
  20.9 0.6 fusion.99
  22.9 0.6 fusion.101
  23.5 1.2 fusion.50
  27.6 0.6 fusion.100
  29.5 0.6 pad_add_fusion
  30.2 0.7 sine_convert_fusion
  32.1 0.4 convolution_reduce_fusion.2
  32.6 0.6 slice_multiply_fusion.1
  33.6 199.3 %all-gather.2.cloned.1.call-done = bf16[2560,2560]{1,0:T(8,128)(2,1)} async-done(((bf16[80,2560]{1,0:T(8,128)(2,1)}), bf16[2560,2560]{1,0:T(8,128)(2,1)}) %all-gather.2.cloned.1.call-update) | async-done | bytes 13107216 | tf_op jit(solution)/shard_map/all_gather | solution.py:133
  233.0 7.4 %multiply_reduce_fusion.2 = (f32[64]{0:T(128)S(1)}, f32[64,2560]{1,0:T(8,128)S(1)}) fusion(bf16[2560,2560]{1,0:T(8,128)(2,1)} %all-gather.2.cloned.1.call-done, bf16[64,2560]{1,0:T(8,128)(2,1)S(1)} %copy-done.3, f32[2560]{0:T(1024)S(1)} %get-tuple-element.41, f32[2560]{0:T(1024)S(1)} %get-tuple-element.42, f32[64]{0:T(128)S(1)} %add_rsqrt_fusion.7, ...), kind=kOutput, calls=%fused_computation.79 | convolution fusion | flops 840171456 | bytes 14111488 | tf_op jit(solution)/shard_map/dot_general | solution.py:87
  240.4 1.0 copy-done.2
  241.4 2.5 multiply_reduce_fusion.4
  244.0 0.9 multiply_multiply_fusion.2
  244.9 1.0 reshape.311
  245.9 1.2 reshape.308
  247.1 2.8 fusion.95
  249.8 1.4 fusion.96
  251.3 112.5 %all-to-all-done = bf16[32,80,2560]{2,1,0:T(8,128)(2,1)} async-done(((bf16[32,80,2560]{2,1,0:T(8,128)(2,1)}), bf16[32,80,2560]{2,1,0:T(8,128)(2,1)}, u32[]{:S(2)}, u32[]{:S(2)}) %all-to-all-start) | async-done | bytes 13107232 | tf_op jit(solution)/shard_map/all_to_all | solution.py:131
  363.8 7.3 %multiply_reduce_fusion.3 = (f32[64]{0:T(128)S(1)}, f32[64,2560]{1,0:T(8,128)S(1)}) fusion(bf16[2560,2560]{1,0:T(8,128)(2,1)} %bitcast.10, bf16[64,2560]{1,0:T(8,128)(2,1)S(1)} %copy-done.3, f32[2560]{0:T(1024)S(1)} %get-tuple-element.41, f32[2560]{0:T(1024)S(1)} %get-tuple-element.42, f32[64]{0:T(128)S(1)} %add_rsqrt_fusion.7, ...), kind=kOutput, calls=%fused_computation.83 | convolution fusion | flops 840171456 | bytes 14111488 | tf_op jit(solution)/shard_map/dot_general | solution.py:86
  371.1 1.0 multiply_multiply_fusion.3
  372.1 1.2 reshape.310
  373.6 0.8 copy-done.5
  375.1 1.8 subtract_convert_fusion.3
  377.5 0.9 pad_maximum_fusion.12
  378.4 3.0 collective-permute-start.1
  381.5 0.4 convolution_reduce_fusion
  381.9 0.6 slice_multiply_fusion
  382.5 1.0 copy_bitcast_fusion.1
  383.5 4.3 collective-permute-start
  387.8 12.2 %collective-permute-done.1 = bf16[2,64,2560]{2,1,0:T(8,128)(2,1)S(1)} collective-permute-done((bf16[2,64,2560]{2,1,0:T(8,128)(2,1)}, bf16[2,64,2560]{2,1,0:T(8,128)(2,1)S(1)}, u32[]{:S(2)}, u32[]{:S(2)}) %collective-permute-start.1) | collective-permute-done | bytes 655392 | tf_op jit(solution)/shard_map/ppermute | solution.py:20
  400.3 3.0 collective-permute-done
  403.7 0.8 copy.25
  404.7 0.8 copy.32
  405.7 0.8 copy.31
  406.5 3.1 fusion.102
  409.6 1.9 fusion.11
  412.0 1.0 copy_bitcast_fusion
  413.0 7.3 %multiply_reduce_fusion.1 = (f32[64]{0:T(128)S(1)}, f32[64,2560]{1,0:T(8,128)S(1)}) fusion(bf16[2560,2560]{1,0:T(8,128)(2,1)} %bitcast.10, bf16[64,2560]{1,0:T(8,128)(2,1)S(1)} %get-tuple-element.6, f32[2560]{0:T(1024)S(1)} %get-tuple-element.38, f32[2560]{0:T(1024)S(1)} %get-tuple-element.39, f32[64]{0:T(128)S(1)} %add_rsqrt_fusion.2, ...), kind=kOutput, calls=%fused_computation.75 | convolution fusion | flops 840171456 | bytes 14111488 | tf_op jit(solution)/shard_map/dot_general | solution.py:163
  420.8 7.3 %multiply_reduce_fusion = (f32[64]{0:T(128)S(1)}, f32[64,2560]{1,0:T(8,128)S(1)}) fusion(bf16[2560,2560]{1,0:T(8,128)(2,1)} %all-gather.2.cloned.1.call-done, bf16[64,2560]{1,0:T(8,128)(2,1)S(1)} %get-tuple-element.6, f32[2560]{0:T(1024)S(1)} %get-tuple-element.38, f32[2560]{0:T(1024)S(1)} %get-tuple-element.39, f32[64]{0:T(128)S(1)} %add_rsqrt_fusion.2, ...), kind=kOutput, calls=%fused_computation.71 | convolution fusion | flops 840171456 | bytes 14111488 | tf_op jit(solution)/shard_map/dot_general | solution.py:164
  428.1 1.0 multiply_multiply_fusion
  429.1 1.2 reshape.313
  430.6 0.5 subtract_convert_fusion.1
  431.1 3.1 fusion.105
  434.2 2.2 fusion.9
  436.4 0.8 fusion.39
  (92 shorter events, 5.8 us)
Async XLA Ops:
  6.5 25.2 %copy-start = (bf16[128,7680]{1,0:T(8,128)(2,1)S(1)}, bf16[128,7680]{1,0:T(8,128)(2,1)}, u32[]{:S(2)}) copy-start(bf16[128,7680]{1,0:T(8,128)(2,1)} %param.17) | copy-start | bytes 5898244
  6.5 226.4 %all-gather.2.cloned.1.call-start = ((), (), s32[]{:S(2)}) async-start(), calls=%async_computation.1 | async-start | bytes 13516800 | tf_op jit(solution)/shard_map/all_gather | solution.py:133
  14.5 6.4 %copy-start.20 = (s32[1,2]{1,0:T(1,128)S(1)}, s32[1,2]{1,0:T(1,128)}, u32[]{:S(2)}) copy-start(s32[1,2]{1,0:T(1,128)} %param.14) | copy-start | bytes 28
  14.5 8.4 %copy-start.19 = (s32[32]{0:T(128)S(1)}, s32[32]{0:T(128)}, u32[]{:S(2)}) copy-start(s32[32]{0:T(128)} %param.12) | copy-start | bytes 388
  14.5 13.2 %copy-start.21 = (s32[1,2]{1,0:T(1,128)S(1)}, s32[1,2]{1,0:T(1,128)}, u32[]{:S(2)}) copy-start(s32[1,2]{1,0:T(1,128)} %param.13) | copy-start | bytes 28
  14.5 16.4 %copy-start.4 = (bf16[64,2560]{1,0:T(8,128)(2,1)S(1)}, bf16[64,2560]{1,0:T(8,128)(2,1)}, u32[]{:S(2)}) copy-start(bf16[64,2560]{1,0:T(8,128)(2,1)} %param.11) | copy-start | bytes 983044
  14.5 16.5 %copy-start.3 = (bf16[64,2560]{1,0:T(8,128)(2,1)S(1)}, bf16[64,2560]{1,0:T(8,128)(2,1)}, u32[]{:S(2)}) copy-start(bf16[64,2560]{1,0:T(8,128)(2,1)} %param.10) | copy-start | bytes 983044
  14.5 349.3 %all-to-all-start = ((bf16[32,80,2560]{2,1,0:T(8,128)(2,1)}), bf16[32,80,2560]{2,1,0:T(8,128)(2,1)}, u32[]{:S(2)}, u32[]{:S(2)}) async-start(bf16[32,80,2560]{2,1,0:T(8,128)(2,1)} %stack.8), calls=%async_computation | async-start | bytes 26214400 | tf_op jit(solution)/shard_map/all_to_all | solution.py:131
  233.0 8.5 %copy-start.2 = (bf16[2560,2560]{1,0:T(8,128)(2,1)S(1)}, bf16[2560,2560]{1,0:T(8,128)(2,1)}, u32[]{:S(2)}) copy-start(bf16[2560,2560]{1,0:T(8,128)(2,1)} %all-gather.2.cloned.1.call-done) | copy-start | bytes 39321604
  241.4 2.6 copy-start.16
  363.8 7.3 %copy-start.15 = (f32[2560]{0:T(1024)S(1)}, f32[2560]{0:T(1024)}, u32[]{:S(2)}) copy-start(f32[2560]{0:T(1024)} %param.18) | copy-start | bytes 30724
  373.3 1.1 copy-start.5
  373.3 1.4 copy-start.6
  373.3 1.6 copy-start.7
  373.3 1.8 copy-start.8
  376.9 4.6 %copy-start.22 = (bf16[64]{0:T(256)(128)(2,1)S(1)}, bf16[64]{0:T(256)(128)(2,1)}, u32[]{:S(2)}) copy-start(bf16[64]{0:T(256)(128)(2,1)} %get-tuple-element.74) | copy-start | bytes 388
  376.9 4.6 %copy-start.23 = (bf16[64]{0:T(256)(128)(2,1)S(1)}, bf16[64]{0:T(256)(128)(2,1)}, u32[]{:S(2)}) copy-start(bf16[64]{0:T(256)(128)(2,1)} %get-tuple-element.75) | copy-start | bytes 388
  378.4 21.6 %collective-permute-start.1 = (bf16[2,64,2560]{2,1,0:T(8,128)(2,1)}, bf16[2,64,2560]{2,1,0:T(8,128)(2,1)S(1)}, u32[]{:S(2)}, u32[]{:S(2)}) collective-permute-start(bf16[2,64,2560]{2,1,0:T(8,128)(2,1)} %pad_maximum_fusion.12), channel_id=1, source_target_pairs={{0,2},{1,3},{2,4},{3,5},{4,6},{5,7},{6,8},{7,9},{8,10},{9,11},{10,... | collective-permute-start | bytes 1966088 | tf_op jit(solution)/shard_map/ppermute | solution.py:20
  383.5 19.8 %collective-permute-start = (bf16[2,64,2560]{2,1,0:T(8,128)(2,1)}, bf16[2,64,2560]{2,1,0:T(8,128)(2,1)S(1)}, u32[]{:S(2)}, u32[]{:S(2)}) collective-permute-start(bf16[2,64,2560]{2,1,0:T(8,128)(2,1)} %pad_maximum_fusion.12), channel_id=1, source_target_pairs={{0,1},{1,2},{2,3},{3,4},{4,5},{5,6},{6,7},{7,8},{8,9},{9,10},{10,1... | collective-permute-start | bytes 1966088 | tf_op jit(solution)/shard_map/ppermute | solution.py:20
  400.3 9.3 %copy-start.13 = (bf16[64,20,128]{2,0,1:T(8,128)(2,1)}, bf16[64,20,128]{2,0,1:T(8,128)(2,1)S(1)}, u32[]{:S(2)}) copy-start(bf16[64,20,128]{2,0,1:T(8,128)(2,1)S(1)} %copy.26) | copy-start | bytes 983044
  403.6 2.9 copy-start.9
  403.6 2.9 copy-start.10
  403.6 2.9 copy-start.11
  403.6 2.9 copy-start.12
  403.6 2.8 copy-start.24
  406.5 3.1 copy-start.14
  409.6 1.9 copy-start.17
  434.2 2.2 copy-start.18
  434.2 3.1 copy-start.1
Sparse Core Ops, SparseCore 0:
  10.2 222.7 all-gather.1
